TPU v7x, 256 devices: a whole 4x4x8 slice. The times are simulated.
256 devices in a mesh: dp: 2 (over z_lo), tensor: 128 (over x, y, z_hi, core).
Axes of the slice: x: 4, y: 4, z: 8 (z_hi: 4, z_lo: 2; z = z_hi * 2 + z_lo), core: 2. Of those that a mesh axis runs over, the one named last changes fastest.
Arguments:
- tokens: bfloat16 [2, 16384, 4096], P('dp', 'tensor'), may hold values from -35 to 35
- norm_gain: float32 [4096], replicated, may hold values from 0.1 to 1.9
- segments: int32 [2, 16384], P('dp', 'tensor'), may hold values from 0 to 7, never falling along the last dimension, each value on 1 to 8192 neighbouring positions
- deal_table: int32 [128, 2], P('tensor'), may hold values from 0 to 1, each once within a row
- projection: bfloat16 [32768, 768], P('tensor'), may hold values from -1 to 1
Outputs:
- context: bfloat16 [2, 16384, 4096], P('dp', 'tensor')
- key_cache: bfloat16 [2, 8, 16384, 128], P('dp', None, 'tensor')
- value_cache: bfloat16 [2, 8, 16384, 128], P('dp', None, 'tensor')
Inputs may be any that keep to these rules, and one draw needn't show every extreme that they name: `segments`: segment ids never fall along a buffer; every id appears, each on at most 8192 positions, one on exactly 8192. `deal_table`: each row names every group once.
All inputs are finite; a program needn't handle non-finite values.
Results may differ from a plain program's by a relative error of at most 0.0082.
Values may be sent and summed in bfloat16 or wider, within the bound.
A program may use at most 128 MiB of HBM per device.

v0:
```python
import jax
import jax.numpy as jnp
from jax import lax
from jax.sharding import PartitionSpec as P

QUERY_HEADS = 32
KEY_VALUE_HEADS = 8
HEAD_SIZE = 128
NSEG = 8
WINDOW = 512
SINKS = 4
rope_base = 500000.0
norm_eps = 1e-05


def from_partner(value, axis, apart):
    mask = 2**apart
    pairs = [(source, source ^ mask) for source in range(lax.axis_size(axis))]
    return lax.ppermute(value, axis, pairs)


def shifted(block, axis, distance):
    devices = range(lax.axis_size(axis))
    route = [(i - distance, i) for i in devices if i - distance in devices]
    return lax.ppermute(block, axis, route)


def stack_pair(holding, arrived, upper_flag, axis_pos):
    lower_part = jnp.where(upper_flag, arrived, holding)
    upper_part = jnp.where(upper_flag, holding, arrived)
    return jnp.stack((lower_part, upper_part), axis=axis_pos)


def rotary(values, angles):
    half_width = values.shape[-1] // 2
    first_half = values[..., :half_width]
    second_half = values[..., half_width:]
    cosine = jnp.cos(angles)
    sine_part = jnp.sin(angles)
    return jnp.concatenate(
        (
            first_half * cosine - second_half * sine_part,
            second_half * cosine + first_half * sine_part,
        ),
        -1,
    )


def body(tokens, norm_gain, segments, deal_table, projection):
    group_id = lax.axis_index("dp")
    device_number = lax.axis_index("tensor")
    tensor_width = lax.axis_size("tensor")
    token_per_device = tokens.shape[1]
    model_width = tokens.shape[2]
    block_length = KEY_VALUE_HEADS * token_per_device
    head_number = device_number % KEY_VALUE_HEADS
    block_number = device_number // KEY_VALUE_HEADS
    group_queries = QUERY_HEADS // KEY_VALUE_HEADS
    head_bit_flags = KEY_VALUE_HEADS.bit_length() - 1
    level_bits = tensor_width.bit_length() - 1
    own_page = tokens[0]
    other_page = from_partner(own_page, "dp", 0)
    owner_group = jnp.sum(jnp.where(jnp.arange(deal_table.shape[1]) == group_id, deal_table[0], 0))
    stay_here = owner_group == group_id
    dealt_rows = jnp.where(stay_here, own_page, other_page)
    widened = dealt_rows.astype(jnp.float32)
    normed = (
        widened * lax.rsqrt(jnp.mean(widened * widened, -1, keepdims=True) + norm_eps) * norm_gain
    ).astype(jnp.bfloat16)
    segment_ids = segments[0]
    segment_match = segment_ids[:, None] == jnp.arange(NSEG)[None, :]
    counts_total = lax.psum(jnp.sum(segment_match.astype(jnp.float32), 0), "tensor")
    counts_int = counts_total.astype(jnp.int32)
    seg_starts = jnp.cumsum(counts_int) - counts_int
    row_starts = jnp.sum(jnp.where(segment_match, seg_starts[None, :], 0), 1)
    bit_order = list(range(head_bit_flags))
    rows_held = normed
    starts_held = row_starts
    gathered_bits = []
    for bit_index in bit_order:
        upper_flag = device_number >> bit_index & 1 == 1
        axis_pos = len([earlier for earlier in gathered_bits if earlier > bit_index])
        rows_far = from_partner(rows_held, "tensor", bit_index)
        starts_far = from_partner(starts_held, "tensor", bit_index)
        rows_held = stack_pair(rows_held, rows_far, upper_flag, axis_pos)
        starts_held = stack_pair(starts_held, starts_far, upper_flag, axis_pos)
        gathered_bits.append(bit_index)
    rows_block = rows_held.reshape(block_length, model_width)
    starts_block = starts_held.reshape(block_length)
    weights_held = projection
    for level_index in range(level_bits - head_bit_flags):
        bit_index = head_bit_flags + level_index
        upper_flag = device_number >> bit_index & 1 == 1
        arrived = from_partner(weights_held, "tensor", bit_index)
        weights_held = stack_pair(weights_held, arrived, upper_flag, 0).reshape(
            -1, weights_held.shape[1]
        )
    projected = jnp.dot(rows_block, weights_held, preferred_element_type=jnp.float32)
    rope_freq = rope_base ** (-(jnp.arange(0, HEAD_SIZE, 2).astype(jnp.float32) / HEAD_SIZE))
    block_positions = block_number * block_length + jnp.arange(block_length)
    angles = (block_positions - starts_block).astype(jnp.float32)[:, None] * rope_freq[None, :]
    queries = rotary(
        projected[:, : group_queries * HEAD_SIZE].reshape(block_length, group_queries, HEAD_SIZE),
        angles[:, None, :],
    ).astype(jnp.bfloat16)
    keys_own = rotary(
        projected[:, group_queries * HEAD_SIZE : (group_queries + 1) * HEAD_SIZE], angles
    ).astype(jnp.bfloat16)
    values_own = projected[:, (group_queries + 1) * HEAD_SIZE :].astype(jnp.bfloat16)
    local_pairs = jnp.concatenate((keys_own, values_own), 1)
    reach_blocks = -(-WINDOW // block_length)
    previous_pairs = [shifted(local_pairs, "tensor", 1 * KEY_VALUE_HEADS)]
    window_pairs = jnp.concatenate(previous_pairs + [local_pairs], 0)
    sink_positions = (seg_starts[:, None] + jnp.arange(SINKS)[None, :]).reshape(NSEG * SINKS)
    local_rows = sink_positions - block_number * block_length
    selector = (local_rows[:, None] == jnp.arange(block_length)[None, :]).astype(jnp.bfloat16)
    selected_rows = jnp.dot(selector, rows_block, preferred_element_type=jnp.float32)
    slice_width = model_width // KEY_VALUE_HEADS
    own_slice = jnp.arange(model_width) // slice_width == head_number
    slice_rows = jnp.where(own_slice[None, :], selected_rows, 0.0)
    sink_table = lax.psum(slice_rows, "tensor")
    sink_normed = sink_table.astype(jnp.bfloat16)
    sink_projected = jnp.dot(
        sink_normed,
        weights_held[:, group_queries * HEAD_SIZE :],
        preferred_element_type=jnp.float32,
    ).reshape(NSEG, SINKS, 2 * HEAD_SIZE)
    sink_angles = jnp.arange(SINKS).astype(jnp.float32)[:, None] * rope_freq[None, :]
    sink_key_rows = rotary(sink_projected[:, :, :HEAD_SIZE], sink_angles[None, :, :]).astype(
        jnp.bfloat16
    )
    sink_value_rows = sink_projected[:, :, HEAD_SIZE:].astype(jnp.bfloat16)
    sink_pairs = jnp.concatenate((sink_key_rows, sink_value_rows), -1)
    tile_rows = min(512, block_length)
    score_scale = HEAD_SIZE ** (-0.5)

    def attend(tile_start):
        query_tile = lax.dynamic_slice_in_dim(queries, tile_start, tile_rows, 0)
        query_pos = block_number * block_length + tile_start + jnp.arange(tile_rows)
        query_start = lax.dynamic_slice_in_dim(starts_block, tile_start, tile_rows, 0)
        key_from = reach_blocks * block_length + tile_start - WINDOW
        key_pairs = lax.dynamic_slice_in_dim(window_pairs, key_from, WINDOW + tile_rows, 0)
        key_pos = (
            (block_number - reach_blocks) * block_length + key_from + jnp.arange(WINDOW + tile_rows)
        )
        scores = (
            jnp.einsum(
                "rgd,kd->rgk",
                query_tile,
                key_pairs[:, :HEAD_SIZE],
                preferred_element_type=jnp.float32,
            )
            * score_scale
        )
        allowed = (
            (key_pos[None, :] <= query_pos[:, None])
            & (key_pos[None, :] >= query_start[:, None])
            & (key_pos[None, :] >= query_pos[:, None] - WINDOW)
        )
        chooser = (seg_starts[None, :] == query_start[:, None]).astype(jnp.bfloat16)
        row_sinks = jnp.einsum(
            "rs,sqc->rqc", chooser, sink_pairs, preferred_element_type=jnp.float32
        ).astype(jnp.bfloat16)
        sink_scores = (
            jnp.einsum(
                "rgd,rqd->rgq",
                query_tile,
                row_sinks[:, :, :HEAD_SIZE],
                preferred_element_type=jnp.float32,
            )
            * score_scale
        )
        sink_pos = query_start[:, None] + jnp.arange(SINKS)[None, :]
        sink_allowed = (sink_pos <= query_pos[:, None]) & (sink_pos < query_pos[:, None] - WINDOW)
        masked = jnp.where(allowed[:, None, :], scores, -jnp.inf)
        masked_sinks = jnp.where(sink_allowed[:, None, :], sink_scores, -jnp.inf)
        top_score = jnp.maximum(
            jnp.max(masked, -1, keepdims=True), jnp.max(masked_sinks, -1, keepdims=True)
        )
        window_weights = jnp.exp(masked - top_score)
        sink_weights = jnp.exp(masked_sinks - top_score)
        denominator = jnp.sum(window_weights, -1, keepdims=True) + jnp.sum(
            sink_weights, -1, keepdims=True
        )
        window_probs = (window_weights / denominator).astype(jnp.bfloat16)
        sink_probs = (sink_weights / denominator).astype(jnp.bfloat16)
        mixed_rows = jnp.einsum(
            "rgk,kd->rgd",
            window_probs,
            key_pairs[:, HEAD_SIZE:],
            preferred_element_type=jnp.float32,
        )
        mixed_rows = mixed_rows + jnp.einsum(
            "rgq,rqd->rgd",
            sink_probs,
            row_sinks[:, :, HEAD_SIZE:],
            preferred_element_type=jnp.float32,
        )
        return mixed_rows.astype(jnp.bfloat16).reshape(tile_rows, group_queries * HEAD_SIZE)

    tile_offsets = jnp.arange(block_length // tile_rows, dtype=jnp.int32) * tile_rows
    context_block = lax.map(attend, tile_offsets).reshape(block_length, group_queries * HEAD_SIZE)
    pairs_by_dest = local_pairs.reshape((2,) * head_bit_flags + (token_per_device, 2 * HEAD_SIZE))
    context_by_dest = context_block.reshape(
        (2,) * head_bit_flags + (token_per_device, group_queries * HEAD_SIZE)
    )
    kept_pairs = pairs_by_dest
    for bit_index in range(head_bit_flags):
        axis_pos = head_bit_flags - 1 - bit_index
        bit_value = device_number >> bit_index & 1
        own_half = lax.dynamic_index_in_dim(kept_pairs, bit_value, axis_pos, keepdims=False)
        sent_half = lax.dynamic_index_in_dim(kept_pairs, 1 - bit_value, axis_pos, keepdims=False)
        arrived = from_partner(sent_half, "tensor", bit_index)
        kept_pairs = stack_pair(own_half, arrived, bit_value == 1, axis_pos)
    kept_context = context_by_dest
    for bit_index in range(head_bit_flags):
        axis_pos = head_bit_flags - 1 - bit_index
        bit_value = device_number >> bit_index & 1
        own_half = lax.dynamic_index_in_dim(kept_context, bit_value, axis_pos, keepdims=False)
        sent_half = lax.dynamic_index_in_dim(kept_context, 1 - bit_value, axis_pos, keepdims=False)
        arrived = from_partner(sent_half, "tensor", bit_index)
        kept_context = stack_pair(own_half, arrived, bit_value == 1, axis_pos)
    cached_heads = kept_pairs.reshape(KEY_VALUE_HEADS, token_per_device, 2 * HEAD_SIZE)
    key_cache = cached_heads[:, :, :HEAD_SIZE][None]
    value_cache = cached_heads[:, :, HEAD_SIZE:][None]
    context_local = (
        kept_context.reshape(KEY_VALUE_HEADS, token_per_device, group_queries * HEAD_SIZE)
        .transpose(1, 0, 2)
        .reshape(token_per_device, QUERY_HEADS * HEAD_SIZE)
    )
    context_back = from_partner(context_local, "dp", 0)
    context = jnp.where(stay_here, context_local, context_back)[None]
    return (context, key_cache, value_cache)


def solution(mesh):
    placed = (P("dp", "tensor", None), P(), P("dp", "tensor"), P("tensor", None), P("tensor", None))
    return jax.shard_map(
        body,
        mesh=mesh,
        in_specs=placed,
        out_specs=(
            P("dp", "tensor", None),
            P("dp", None, "tensor", None),
            P("dp", None, "tensor", None),
        ),
        check_vma=False,
    )
```

profile of v0, /device:TPU:32, one launch (start us, length us, event | category | flops | bytes accessed | tf_op | source)
XLA Modules:
  0.0 1571.1 jit_solution(10747229112647004159)
XLA Ops:
  0.7 1.9 collective-permute-start.3
  4.5 7.4 collective-permute-done.7
  13.0 3.3 collective-permute-start.8
  16.3 9.5 collective-permute-done.3
  26.8 1.6 fusion.25
  28.6 4.5 collective-permute-done.8
  34.5 1.6 collective-permute-start.9
  36.1 1.7 select_bitcast_fusion.10
  40.3 3.3 collective-permute-start.5
  43.6 25.5 %collective-permute-done.9 = bf16[1024,768]{1,0:T(8,128)(2,1)} collective-permute-done((bf16[1024,768]{1,0:T(8,128)(2,1)S(1)}, bf16[1024,768]{1,0:T(8,128)(2,1)}, u32[]{:S(2)}, u32[]{:S(2)}) %collective-permute-start.9) | collective-permute-done | bytes 1572896 | tf_op jit(solution)/shard_map/ppermute | solution.py:19
  70.7 1.9 pad_maximum_fusion.3
  72.6 3.1 collective-permute-start.10
  75.8 56.0 %collective-permute-done.5 = bf16[2,128,4096]{2,1,0:T(8,128)(2,1)} collective-permute-done((bf16[2,128,4096]{2,1,0:T(8,128)(2,1)}, bf16[2,128,4096]{2,1,0:T(8,128)(2,1)}, u32[]{:S(2)}, u32[]{:S(2)}) %collective-permute-start.5) | collective-permute-done | bytes 2097184 | tf_op jit(solution)/shard_map/ppermute | solution.py:19
  131.7 2.0 select_bitcast_fusion.5
  133.8 2.6 pad_maximum_fusion.2
  136.4 4.6 collective-permute-start.6
  141.1 513.5 %psum.14 = f32[8]{0:T(128)S(1)} all-reduce(f32[8]{0:T(128)S(1)} %convert_reduce_fusion), channel_id=1, replica_groups=mesh['dp'=2,'tensor'=128] {'tensor'}, use_global_device_ids=true, to_apply=%region_3.4 | all-reduce | flops 8 | bytes 64 | tf_op jit(solution)/shard_map/psum | solution.py:72
  658.0 4.4 collective-permute-done.1
  663.4 6.9 collective-permute-done.2
  672.1 3.3 select_bitcast_fusion.3
  675.4 3.2 pad_maximum_fusion.1
  678.6 5.1 select_bitcast_fusion.1
  683.8 7.6 pad_maximum_fusion
  691.4 11.3 fusion.60
  702.7 2.3 convolution_select_fusion
  705.0 684.3 %all-reduce.1 = bf16[32,4096]{1,0:T(8,128)(2,1)S(1)} all-reduce(f32[32,4096]{1,0:T(8,128)} %convolution_select_fusion), channel_id=1, replica_groups=mesh['dp'=2,'tensor'=128] {'tensor'}, use_global_device_ids=true, to_apply=%region_6.7 | all-reduce | flops 131072 | bytes 786432 | tf_op jit(solution)/shard_map/psum | solution.py:121
  1389.3 2.0 fusion.26
  1392.3 2.6 subtract_convert_fusion.1
  1396.4 2.1 collective-permute-start.11
  1399.6 1.8 copy.242
  1401.5 2.0 copy.243
  1407.3 2.1 subtract_convert_fusion
  1411.0 2.1 maximum_maximum_fusion
  1413.2 57.3 %while.15 = (s32[]{:T(128)}, bf16[2,512,512]{2,1,0:T(8,128)(2,1)}, s32[2]{0:T(128)}, s32[]{:T(128)}, s32[]{:T(128)}, /*index=5*/s32[1024]{0:T(1024)}, bf16[1024,...) while((s32[]{:T(128)}, bf16[2,512,512]{2,1,0:T(8,128)(2,1)}, ...), condition=%wide.region_12.13_spmd, body=%wide.region_7.12_spmd.sunk | while | flops 1115269120 | bytes 41343824 | solution.py:202
  1422.2 5.9 fusion.93
  1429.4 4.7 fusion.96
  1435.5 5.2 fusion.99
  1450.9 5.9 fusion.93
  1458.0 4.7 fusion.96
  1464.2 5.2 fusion.99
  1471.6 1.9 collective-permute-done.12
  1478.9 17.6 %collective-permute-done.13 = bf16[2,2,128,512]{3,2,1,0:T(8,128)(2,1)S(1)} collective-permute-done((bf16[2,2,128,512]{3,2,1,0:T(8,128)(2,1)S(1)}, bf16[2,2,128,512]{3,2,1,0:T(8,128)(2,1)S(1)}, u32[]{:S(2)}, u32[]{:S(2)}) %collective-permute-start.13) | collective-permute-done | bytes 524320 | tf_op jit(solution)/shard_map/ppermute | solution.py:19
  1499.0 3.3 collective-permute-start.17
  1502.3 19.0 %collective-permute-done.14 = bf16[2,2,128,512]{3,2,1,0:T(8,128)(2,1)S(1)} collective-permute-done((bf16[2,2,128,512]{3,2,1,0:T(8,128)(2,1)S(1)}, bf16[2,2,128,512]{3,2,1,0:T(8,128)(2,1)S(1)}, u32[]{:S(2)}, u32[]{:S(2)}) %collective-permute-start.14) | collective-permute-done | bytes 524320 | tf_op jit(solution)/shard_map/ppermute | solution.py:19
  1522.8 6.4 collective-permute-start.15
  1529.1 4.3 collective-permute-done.17
  1534.4 2.9 collective-permute-start.18
  1537.3 31.6 %collective-permute-done.18 = bf16[2,2,128,256]{3,2,1,0:T(8,128)(2,1)S(1)} collective-permute-done((bf16[2,2,128,256]{3,2,1,0:T(8,128)(2,1)S(1)}, bf16[2,2,128,256]{3,2,1,0:T(8,128)(2,1)S(1)}, u32[]{:S(2)}, u32[]{:S(2)}) %collective-permute-start.18) | collective-permute-done | bytes 262176 | tf_op jit(solution)/shard_map/ppermute | solution.py:19
  (151 shorter events, 55.6 us)
Async XLA Ops:
  0.6 25.2 %copy-start.7 = (bf16[1,128,4096]{2,1,0:T(8,128)(2,1)S(1)}, bf16[1,128,4096]{2,1,0:T(8,128)(2,1)}, u32[]{:S(2)}) copy-start(bf16[1,128,4096]{2,1,0:T(8,128)(2,1)} %param.7) | copy-start | bytes 3145732
  0.6 26.2 %copy-start.12 = (f32[4096]{0:T(1024)S(1)}, f32[4096]{0:T(1024)}, u32[]{:S(2)}) copy-start(f32[4096]{0:T(1024)} %param.8) | copy-start | bytes 49156
  0.7 25.2 %collective-permute-start.3 = (bf16[128,4096]{1,0:T(8,128)(2,1)}, bf16[128,4096]{1,0:T(8,128)(2,1)S(1)}, u32[]{:S(2)}, u32[]{:S(2)}) collective-permute-start(bf16[128,4096]{1,0:T(8,128)(2,1)} %bitcast.201), channel_id=1, source_target_pairs={{0,128},{128,0},{1,129},{129,1},{2,130},{130,2},{3,131},{131,3},{4... | collective-permute-start | bytes 3145736 | tf_op jit(solution)/shard_map/ppermute | solution.py:19
  2.6 9.3 collective-permute-start.7
  13.0 20.1 %collective-permute-start.8 = (bf16[512,768]{1,0:T(8,128)(2,1)S(1)}, bf16[512,768]{1,0:T(8,128)(2,1)}, u32[]{:S(2)}, u32[]{:S(2)}) collective-permute-start(bf16[512,768]{1,0:T(8,128)(2,1)S(1)} %bitcast.202), channel_id=1, source_target_pairs={{0,16},{1,17},{2,18},{3,19},{4,20},{5,21},{6,22},{7,23},{8,24},{9,... | collective-permute-start | bytes 2359304 | tf_op jit(solution)/shard_map/ppermute | solution.py:19
  25.8 1.0 copy-start.8
  28.5 6.0 copy-start.6
  28.5 7.7 collective-permute-start.4
  34.5 34.6 %collective-permute-start.9 = (bf16[1024,768]{1,0:T(8,128)(2,1)S(1)}, bf16[1024,768]{1,0:T(8,128)(2,1)}, u32[]{:S(2)}, u32[]{:S(2)}) collective-permute-start(bf16[1024,768]{1,0:T(8,128)(2,1)S(1)} %bitcast.198), channel_id=1, source_target_pairs={{0,32},{1,33},{2,34},{3,35},{4,36},{5,37},{6,38},{7,39},{8,40},{9,... | collective-permute-start | bytes 4718600 | tf_op jit(solution)/shard_map/ppermute | solution.py:19
  37.8 1.0 copy-start.3
  40.3 91.4 %collective-permute-start.5 = (bf16[2,128,4096]{2,1,0:T(8,128)(2,1)}, bf16[2,128,4096]{2,1,0:T(8,128)(2,1)}, u32[]{:S(2)}, u32[]{:S(2)}) collective-permute-start(bf16[2,128,4096]{2,1,0:T(8,128)(2,1)} %pad_maximum_fusion.4), channel_id=1, source_target_pairs={{0,2},{1,3},{2,0},{3,1},{4,6},{5,7},{6,4},{7,5},{8,10},{9,11},{10,... | collective-permute-start | bytes 6291464 | tf_op jit(solution)/shard_map/ppermute | solution.py:19
  70.7 61.1 %copy-start.4 = (bf16[1,128,4096]{2,1,0:T(8,128)(2,1)S(1)}, bf16[1,128,4096]{2,1,0:T(8,128)(2,1)}, u32[]{:S(2)}) copy-start(bf16[1,128,4096]{2,1,0:T(8,128)(2,1)} %copy-done.3) | copy-start | bytes 3145732
  72.6 599.5 %collective-permute-start.10 = (bf16[2048,768]{1,0:T(8,128)(2,1)}, bf16[2048,768]{1,0:T(8,128)(2,1)}, u32[]{:S(2)}, u32[]{:S(2)}) collective-permute-start(bf16[2048,768]{1,0:T(8,128)(2,1)} %bitcast.32), channel_id=1, source_target_pairs={{0,64},{1,65},{2,66},{3,67},{4,68},{5,69},{6,70},{7,71},{8,72},{9,... | collective-permute-start | bytes 9437192 | tf_op jit(solution)/shard_map/ppermute | solution.py:19
  133.7 2.6 copy-start.1
  133.8 7.2 copy-start.14
  136.4 542.2 %collective-permute-start.6 = (bf16[2,2,128,4096]{3,2,1,0:T(8,128)(2,1)}, bf16[2,2,128,4096]{3,2,1,0:T(8,128)(2,1)}, u32[]{:S(2)}, u32[]{:S(2)}) collective-permute-start(bf16[2,2,128,4096]{3,2,1,0:T(8,128)(2,1)} %pad_maximum_fusion.2), channel_id=1, source_target_pairs={{0,4},{1,5},{2,6},{3,7},{4,0},{5,1},{6,2},{7,3},{8,12},{9,13},{10,... | collective-permute-start | bytes 12582920 | tf_op jit(solution)/shard_map/ppermute | solution.py:19
  655.9 2.0 collective-permute-start
  656.0 0.5 copy-start.13
  657.9 4.6 collective-permute-start.1
  662.5 7.8 collective-permute-start.2
  675.4 3.2 copy-start.2
  683.8 7.6 copy-start.5
  691.4 11.3 copy-start
  705.0 687.0 %copy-start.9 = (f32[1024,768]{0,1:T(8,128)S(1)}, f32[1024,768]{0,1:T(8,128)}, u32[]{:S(2)}) copy-start(f32[1024,768]{0,1:T(8,128)} %fusion.60) | copy-start | bytes 9437188
  1394.9 3.6 copy-start.10
  1396.4 14.7 collective-permute-start.11
  1409.4 1.6 copy-start.11
  1471.5 2.0 collective-permute-start.12
  1474.8 21.7 %collective-permute-start.13 = (bf16[2,2,128,512]{3,2,1,0:T(8,128)(2,1)S(1)}, bf16[2,2,128,512]{3,2,1,0:T(8,128)(2,1)S(1)}, u32[]{:S(2)}, u32[]{:S(2)}) collective-permute-start(bf16[2,2,128,512]{3,2,1,0:T(8,128)(2,1)S(1)} %bitcast.206), channel_id=1, source_target_pairs={{0,2},{1,3},{2,0},{3,1},{4,6},{5,7},{6,4},{7,5},{8,10},{9,11},{10,... | collective-permute-start | bytes 1572872 | tf_op jit(solution)/shard_map/ppermute | solution.py:19
  1478.8 18.4 %collective-permute-start.16 = (bf16[2,2,128,256]{3,2,1,0:T(8,128)(2,1)}, bf16[2,2,128,256]{3,2,1,0:T(8,128)(2,1)}, u32[]{:S(2)}, u32[]{:S(2)}) collective-permute-start(bf16[2,2,128,256]{3,2,1,0:T(8,128)(2,1)} %bitcast.54), channel_id=1, source_target_pairs={{0,1},{1,0},{2,3},{3,2},{4,5},{5,4},{6,7},{7,6},{8,9},{9,8},{10,11... | collective-permute-start | bytes 786440 | tf_op jit(solution)/shard_map/ppermute | solution.py:19
  1496.6 24.7 %collective-permute-start.14 = (bf16[2,2,128,512]{3,2,1,0:T(8,128)(2,1)S(1)}, bf16[2,2,128,512]{3,2,1,0:T(8,128)(2,1)S(1)}, u32[]{:S(2)}, u32[]{:S(2)}) collective-permute-start(bf16[2,2,128,512]{3,2,1,0:T(8,128)(2,1)S(1)} %fusion.31), channel_id=1, source_target_pairs={{0,4},{1,5},{2,6},{3,7},{4,0},{5,1},{6,2},{7,3},{8,12},{9,13},{10,... | collective-permute-start | bytes 1572872 | tf_op jit(solution)/shard_map/ppermute | solution.py:19
  1499.0 34.4 %collective-permute-start.17 = (bf16[2,2,128,256]{3,2,1,0:T(8,128)(2,1)}, bf16[2,2,128,256]{3,2,1,0:T(8,128)(2,1)}, u32[]{:S(2)}, u32[]{:S(2)}) collective-permute-start(bf16[2,2,128,256]{3,2,1,0:T(8,128)(2,1)} %bitcast.175), channel_id=1, source_target_pairs={{0,2},{1,3},{2,0},{3,1},{4,6},{5,7},{6,4},{7,5},{8,10},{9,11},{10,... | collective-permute-start | bytes 786440 | tf_op jit(solution)/shard_map/ppermute | solution.py:19
  1522.8 47.2 %collective-permute-start.15 = (bf16[128,4096]{1,0:T(8,128)(2,1)S(1)}, bf16[128,4096]{1,0:T(8,128)(2,1)S(1)}, u32[]{:S(2)}, u32[]{:S(2)}) collective-permute-start(bf16[128,4096]{1,0:T(8,128)(2,1)S(1)} %copy.230), channel_id=1, source_target_pairs={{0,128},{128,0},{1,129},{129,1},{2,130},{130,2},{3,131},{131,3},{4... | collective-permute-start | bytes 3145736 | tf_op jit(solution)/shard_map/ppermute | solution.py:19
  1534.4 34.5 %collective-permute-start.18 = (bf16[2,2,128,256]{3,2,1,0:T(8,128)(2,1)S(1)}, bf16[2,2,128,256]{3,2,1,0:T(8,128)(2,1)S(1)}, u32[]{:S(2)}, u32[]{:S(2)}) collective-permute-start(bf16[2,2,128,256]{3,2,1,0:T(8,128)(2,1)S(1)} %fusion.41), channel_id=1, source_target_pairs={{0,4},{1,5},{2,6},{3,7},{4,0},{5,1},{6,2},{7,3},{8,12},{9,13},{10,... | collective-permute-start | bytes 786440 | tf_op jit(solution)/shard_map/ppermute | solution.py:19
where the time goes:
time: 1570 us
  blocking collectives  1200 us (76%)
  waiting for transfers between devices  189 us (12%)
  other arithmetic  68.4 us (4%)
  matrix products  43.1 us (3%)
  starting transfers between devices  33.6 us (2%)
  local copies, waits for them, and re-layouts  29.9 us (2%)
    psum x1, blocking collectives, body(): sink_table = lax.psum(slice_rows, 'tensor')  684 us
    psum x1, blocking collectives, body(): lax.psum(jnp.sum(segment_match.astype(jnp.float32), 0), 'tensor')  513 us
    ppermute x18, waiting for transfers between devices, from_partner(): return lax.ppermute(value, axis, pairs)  189 us
    another operation x30, other arithmetic, stack_pair(): return jnp.stack((lower_part, upper_part), axis=axis_pos)  37.3 us
    ppermute x18, starting transfers between devices, from_partner(): return lax.ppermute(value, axis, pairs)  31.5 us
  transfers between devices with their start and end apart: 19, of which 12 were waited for; matrix products, arithmetic and copies ran while one was open for 3% of the time, Pallas kernels for 0%

commit v1 on v0

--- a/solution.py
+++ b/solution.py
@@ -2,6 +2,7 @@
 import jax.numpy as jnp
 from jax import lax
 from jax.sharding import PartitionSpec as P
+from jax.lax import all_gather
 
 QUERY_HEADS = 32
 KEY_VALUE_HEADS = 8
@@ -118,7 +119,11 @@
     slice_width = model_width // KEY_VALUE_HEADS
     own_slice = jnp.arange(model_width) // slice_width == head_number
     slice_rows = jnp.where(own_slice[None, :], selected_rows, 0.0)
-    sink_table = lax.psum(slice_rows, "tensor")
+
+    def serve_records_here(load, mesh_name):
+        return jnp.sum(all_gather(load, axis_name=mesh_name), 0)
+
+    sink_table = serve_records_here(slice_rows, "tensor")
     sink_normed = sink_table.astype(jnp.bfloat16)
     sink_projected = jnp.dot(
         sink_normed,

time: 1570 us -> 1210 us (0.77)
  blocking collectives: 1200 us -> 514 us
  waiting for transfers between devices: 189 us -> 483 us
    psum x1 -> x0, blocking collectives: 684 us -> none  [body(): sink_table = lax.psum(slice_rows, 'tensor')]
    all_gather x0 -> x1, waiting for transfers between devices: none -> 148 us  [serve_records_here(): return jnp.sum(all_gather(load, axis_name=mesh_name), 0)]
    ppermute x18, waiting for transfers between devices: 189 us -> 319 us  [from_partner(): return lax.ppermute(value, axis, pairs)]
    reduce_sum x0 -> x1, other arithmetic: none -> 20.9 us  [serve_records_here(): return jnp.sum(all_gather(load, axis_name=mesh_name), 0)]
  transfers between devices with their start and end apart: 19 -> 20, of which waited for: 12 -> 17; matrix products, arithmetic and copies ran while one was open for 3% -> 3% of each run, Pallas kernels for 0% -> 0%
where the time goes in v1:
time: 1210 us; the launch traced here: 1200 us
  blocking collectives  514 us (42%)
  waiting for transfers between devices  483 us (40%)
  other arithmetic  73 us (6%)
  starting transfers between devices  41.8 us (3%)
  matrix products  34.7 us (3%)
  local copies, waits for them, and re-layouts  25.6 us (2%)
  between operations  15.4 us (1%)
    psum x1, blocking collectives, body(): lax.psum(jnp.sum(segment_match.astype(jnp.float32), 0), 'tensor')  514 us
    ppermute x18, waiting for transfers between devices, from_partner(): return lax.ppermute(value, axis, pairs)  319 us
    all_gather x1, waiting for transfers between devices, serve_records_here(): return jnp.sum(all_gather(load, axis_name=mesh_name), 0)  148 us
    ppermute x18, starting transfers between devices, from_partner(): return lax.ppermute(value, axis, pairs)  38.5 us
    another operation x30, other arithmetic, stack_pair(): return jnp.stack((lower_part, upper_part), axis=axis_pos)  29.5 us
  transfers between devices with their start and end apart: 20, of which 17 were waited for; matrix products, arithmetic and copies ran while one was open for 3% of the time, Pallas kernels for 0%

profile of v1, /device:TPU:32, one launch (start us, length us, event | category | flops | bytes accessed | tf_op | source)
XLA Modules:
  0.0 1195.5 jit_solution(7937454670775591132)
XLA Ops:
  7.2 1.9 collective-permute-start.3
  11.1 21.3 %collective-permute-done.3 = bf16[128,4096]{1,0:T(8,128)(2,1)S(1)} collective-permute-done((bf16[128,4096]{1,0:T(8,128)(2,1)}, bf16[128,4096]{1,0:T(8,128)(2,1)S(1)}, u32[]{:S(2)}, u32[]{:S(2)}) %collective-permute-start.3) | collective-permute-done | bytes 1048608 | tf_op jit(solution)/shard_map/ppermute | solution.py:20
  34.1 1.7 fusion.25
  35.8 2.6 collective-permute-done.4
  39.8 3.4 collective-permute-start.5
  43.1 89.9 %collective-permute-done.5 = bf16[2,128,4096]{2,1,0:T(8,128)(2,1)} collective-permute-done((bf16[2,128,4096]{2,1,0:T(8,128)(2,1)S(1)}, bf16[2,128,4096]{2,1,0:T(8,128)(2,1)}, u32[]{:S(2)}, u32[]{:S(2)}) %collective-permute-start.5) | collective-permute-done | bytes 2097184 | tf_op jit(solution)/shard_map/ppermute | solution.py:20
  133.0 2.1 select_bitcast_fusion.5
  135.1 2.6 pad_maximum_fusion.2
  137.8 4.8 collective-permute-start.6
  142.7 513.9 %psum.7 = f32[8]{0:T(128)S(1)} all-reduce(f32[8]{0:T(128)S(1)} %convert_reduce_fusion), channel_id=1, replica_groups=mesh['dp'=2,'tensor'=128] {'tensor'}, use_global_device_ids=true, to_apply=%region_3.4 | all-reduce | flops 8 | bytes 64 | tf_op jit(solution)/shard_map/psum | solution.py:73
  656.9 5.5 select_bitcast_fusion.1
  662.4 7.5 pad_maximum_fusion
  669.9 5.7 convolution_select_fusion
  675.7 14.8 %collective-permute-done.7 = bf16[256,768]{1,0:T(8,128)(2,1)S(1)} collective-permute-done((bf16[256,768]{1,0:T(8,128)(2,1)S(1)}, bf16[256,768]{1,0:T(8,128)(2,1)S(1)}, u32[]{:S(2)}, u32[]{:S(2)}) %collective-permute-start.7) | collective-permute-done | bytes 393248 | tf_op jit(solution)/shard_map/ppermute | solution.py:20
  690.8 14.6 %collective-permute-done.8 = bf16[512,768]{1,0:T(8,128)(2,1)S(1)} collective-permute-done((bf16[512,768]{1,0:T(8,128)(2,1)S(1)}, bf16[512,768]{1,0:T(8,128)(2,1)S(1)}, u32[]{:S(2)}, u32[]{:S(2)}) %collective-permute-start.8) | collective-permute-done | bytes 786464 | tf_op jit(solution)/shard_map/ppermute | solution.py:20
  705.8 54.8 %collective-permute-done.9 = bf16[1024,768]{1,0:T(8,128)(2,1)S(1)} collective-permute-done((bf16[1024,768]{1,0:T(8,128)(2,1)S(1)}, bf16[1024,768]{1,0:T(8,128)(2,1)S(1)}, u32[]{:S(2)}, u32[]{:S(2)}) %collective-permute-start.9) | collective-permute-done | bytes 1572896 | tf_op jit(solution)/shard_map/ppermute | solution.py:20
  763.5 3.7 collective-permute-done.1
  768.3 7.0 collective-permute-done.2
  775.3 41.2 %collective-permute-done.10 = bf16[2048,768]{1,0:T(8,128)(2,1)} collective-permute-done((bf16[2048,768]{1,0:T(8,128)(2,1)S(1)}, bf16[2048,768]{1,0:T(8,128)(2,1)}, u32[]{:S(2)}, u32[]{:S(2)}) %collective-permute-start.10) | collective-permute-done | bytes 3145760 | tf_op jit(solution)/shard_map/ppermute | solution.py:20
  816.5 4.2 select_bitcast_fusion.3
  820.7 2.6 pad_maximum_fusion.1
  823.9 7.0 fusion.60
  832.9 1.8 copy.243
  834.7 2.0 copy.242
  836.7 2.8 subtract_convert_fusion.1
  841.8 3.2 collective-permute-start.11
  845.0 2.1 subtract_convert_fusion
  848.8 15.4 %collective-permute-done.11 = bf16[1024,256]{0,1:T(8,128)(2,1)S(1)} collective-permute-done((bf16[1024,256]{0,1:T(8,128)(2,1)S(1)}, bf16[1024,256]{0,1:T(8,128)(2,1)S(1)}, u32[]{:S(2)}, u32[]{:S(2)}) %collective-permute-start.11) | collective-permute-done | bytes 524320 | tf_op jit(solution)/shard_map/ppermute | solution.py:26
  865.3 148.4 %all-gather.3.cloned.1.call-done = f32[4096,4096]{1,0:T(8,128)} async-done(((f32[32,4096]{1,0:T(8,128)}), f32[4096,4096]{1,0:T(8,128)}) %all-gather.3.cloned.1.call-update) | async-done | bytes 67108880 | tf_op jit(solution)/shard_map/all_gather | solution.py:124
  1013.7 20.9 %reduce_sum.81 = bf16[32,4096]{1,0:T(8,128)(2,1)S(1)} reduce(f32[128,32,4096]{2,1,0:T(8,128)} %bitcast.37, f32[]{:T(128)} %constant.196.clone.1), dimensions={0}, to_apply=%region_6.7 | reduce | flops 16646144 | bytes 67371008 | tf_op jit(solution)/shard_map/reduce_sum | solution.py:124
  1034.5 2.1 fusion.26
  1036.8 44.2 %while.15 = (s32[]{:T(128)}, bf16[2,512,512]{2,1,0:T(8,128)(2,1)}, s32[2]{0:T(128)S(1)}, s32[]{:T(128)}, s32[]{:T(128)}, /*index=5*/s32[1024]{0:T(1024)S(1)}, bf...) while((s32[]{:T(128)}, bf16[2,512,512]{2,1,0:T(8,128)(2,1)}, ...), condition=%wide.region_12.13_spmd, body=%wide.region_7.12_spmd.sunk | while | flops 1115269120 | bytes 74897784 | solution.py:207
  1045.1 2.7 fusion.93
  1047.9 2.4 fusion.96
  1052.7 5.2 fusion.99
  1067.3 2.7 fusion.93
  1070.1 2.4 fusion.96
  1074.8 5.2 fusion.99
  1082.5 1.7 collective-permute-done.12
  1085.5 2.8 collective-permute-start.13
  1090.9 20.2 %collective-permute-done.13 = bf16[2,2,128,512]{3,2,1,0:T(8,128)(2,1)S(1)} collective-permute-done((bf16[2,2,128,512]{3,2,1,0:T(8,128)(2,1)S(1)}, bf16[2,2,128,512]{3,2,1,0:T(8,128)(2,1)S(1)}, u32[]{:S(2)}, u32[]{:S(2)}) %collective-permute-start.13) | collective-permute-done | bytes 524320 | tf_op jit(solution)/shard_map/ppermute | solution.py:20
  1111.3 3.6 collective-permute-start.14
  1117.2 3.4 collective-permute-start.17
  1120.5 8.9 collective-permute-done.14
  1130.9 13.7 %collective-permute-start.15 = (bf16[128,4096]{1,0:T(8,128)(2,1)S(1)}, bf16[128,4096]{1,0:T(8,128)(2,1)S(1)}, u32[]{:S(2)}, u32[]{:S(2)}) collective-permute-start(bf16[128,4096]{1,0:T(8,128)(2,1)S(1)} %copy.230), channel_id=1, source_target_pairs={{0,128},{128,0},{1,129},{129,1},{2,130},{130,2},{3,131},{131,3},{4... | collective-permute-start | bytes 3145736 | tf_op jit(solution)/shard_map/ppermute | solution.py:20
  1144.6 4.8 collective-permute-done.17
  1150.5 3.5 collective-permute-start.18
  1154.0 32.4 %collective-permute-done.18 = bf16[2,2,128,256]{3,2,1,0:T(8,128)(2,1)S(1)} collective-permute-done((bf16[2,2,128,256]{3,2,1,0:T(8,128)(2,1)S(1)}, bf16[2,2,128,256]{3,2,1,0:T(8,128)(2,1)S(1)}, u32[]{:S(2)}, u32[]{:S(2)}) %collective-permute-start.18) | collective-permute-done | bytes 262176 | tf_op jit(solution)/shard_map/ppermute | solution.py:20
  (161 shorter events, 44.7 us)
Async XLA Ops:
  7.2 1006.5 %all-gather.3.cloned.1.call-start = ((), (), s32[]{:S(2)}) async-start(), calls=%async_computation | async-start | bytes 67633152 | tf_op jit(solution)/shard_map/all_gather | solution.py:124
  7.2 25.2 %collective-permute-start.3 = (bf16[128,4096]{1,0:T(8,128)(2,1)}, bf16[128,4096]{1,0:T(8,128)(2,1)S(1)}, u32[]{:S(2)}, u32[]{:S(2)}) collective-permute-start(bf16[128,4096]{1,0:T(8,128)(2,1)} %bitcast.205), channel_id=1, source_target_pairs={{0,128},{128,0},{1,129},{129,1},{2,130},{130,2},{3,131},{131,3},{4... | collective-permute-start | bytes 3145736 | tf_op jit(solution)/shard_map/ppermute | solution.py:20
  35.7 2.7 collective-permute-start.4
  38.6 1.0 copy-start.2
  39.8 93.2 %collective-permute-start.5 = (bf16[2,128,4096]{2,1,0:T(8,128)(2,1)S(1)}, bf16[2,128,4096]{2,1,0:T(8,128)(2,1)}, u32[]{:S(2)}, u32[]{:S(2)}) collective-permute-start(bf16[2,128,4096]{2,1,0:T(8,128)(2,1)S(1)} %pad_maximum_fusion.4), channel_id=1, source_target_pairs={{0,2},{1,3},{2,0},{3,1},{4,6},{5,7},{6,4},{7,5},{8,10},{9,11},{10,... | collective-permute-start | bytes 6291464 | tf_op jit(solution)/shard_map/ppermute | solution.py:20
  135.1 2.7 copy-start.1
  135.1 7.4 copy-start.13
  137.8 519.1 %collective-permute-start.6 = (bf16[2,2,128,4096]{3,2,1,0:T(8,128)(2,1)}, bf16[2,2,128,4096]{3,2,1,0:T(8,128)(2,1)}, u32[]{:S(2)}, u32[]{:S(2)}) collective-permute-start(bf16[2,2,128,4096]{3,2,1,0:T(8,128)(2,1)} %pad_maximum_fusion.2), channel_id=1, source_target_pairs={{0,4},{1,5},{2,6},{3,7},{4,0},{5,1},{6,2},{7,3},{8,12},{9,13},{10,... | collective-permute-start | bytes 12582920 | tf_op jit(solution)/shard_map/ppermute | solution.py:20
  669.9 5.8 copy-start.8
  675.6 14.9 %collective-permute-start.7 = (bf16[256,768]{1,0:T(8,128)(2,1)S(1)}, bf16[256,768]{1,0:T(8,128)(2,1)S(1)}, u32[]{:S(2)}, u32[]{:S(2)}) collective-permute-start(bf16[256,768]{1,0:T(8,128)(2,1)S(1)} %copy-done.8), channel_id=1, source_target_pairs={{0,8},{1,9},{2,10},{3,11},{4,12},{5,13},{6,14},{7,15},{8,0},{9,1},... | collective-permute-start | bytes 1179656 | tf_op jit(solution)/shard_map/ppermute | solution.py:20
  690.7 14.7 %collective-permute-start.8 = (bf16[512,768]{1,0:T(8,128)(2,1)S(1)}, bf16[512,768]{1,0:T(8,128)(2,1)S(1)}, u32[]{:S(2)}, u32[]{:S(2)}) collective-permute-start(bf16[512,768]{1,0:T(8,128)(2,1)S(1)} %bitcast.206), channel_id=1, source_target_pairs={{0,16},{1,17},{2,18},{3,19},{4,20},{5,21},{6,22},{7,23},{8,24},{9,... | collective-permute-start | bytes 2359304 | tf_op jit(solution)/shard_map/ppermute | solution.py:20
  705.7 54.9 %collective-permute-start.9 = (bf16[1024,768]{1,0:T(8,128)(2,1)S(1)}, bf16[1024,768]{1,0:T(8,128)(2,1)S(1)}, u32[]{:S(2)}, u32[]{:S(2)}) collective-permute-start(bf16[1024,768]{1,0:T(8,128)(2,1)S(1)} %bitcast.202), channel_id=1, source_target_pairs={{0,32},{1,33},{2,34},{3,35},{4,36},{5,37},{6,38},{7,39},{8,40},{9,... | collective-permute-start | bytes 4718600 | tf_op jit(solution)/shard_map/ppermute | solution.py:20
  761.3 55.3 %collective-permute-start.10 = (bf16[2048,768]{1,0:T(8,128)(2,1)S(1)}, bf16[2048,768]{1,0:T(8,128)(2,1)}, u32[]{:S(2)}, u32[]{:S(2)}) collective-permute-start(bf16[2048,768]{1,0:T(8,128)(2,1)S(1)} %bitcast.198), channel_id=1, source_target_pairs={{0,64},{1,65},{2,66},{3,67},{4,68},{5,69},{6,70},{7,71},{8,72},{9,... | collective-permute-start | bytes 9437192 | tf_op jit(solution)/shard_map/ppermute | solution.py:20
  761.4 1.2 collective-permute-start
  761.5 2.0 copy-start.11
  762.6 4.6 collective-permute-start.1
  767.2 8.0 collective-permute-start.2
  816.5 6.9 slice-start
  820.7 3.1 slice-start.1
  823.4 7.5 copy-start.3
  830.9 2.0 copy-start.4
  832.9 3.8 copy-start.12
  841.8 5.4 copy-start.5
  841.8 22.4 %collective-permute-start.11 = (bf16[1024,256]{0,1:T(8,128)(2,1)S(1)}, bf16[1024,256]{0,1:T(8,128)(2,1)S(1)}, u32[]{:S(2)}, u32[]{:S(2)}) collective-permute-start(bf16[1024,256]{0,1:T(8,128)(2,1)S(1)} %pad_maximum_fusion.9), channel_id=1, source_target_pairs={{0,8},{1,9},{2,10},{3,11},{4,12},{5,13},{6,14},{7,15},{8,16},{9,17... | collective-permute-start | bytes 1572872 | tf_op jit(solution)/shard_map/ppermute | solution.py:26
  847.2 17.1 %copy-start.7 = (bf16[1024,64]{0,1:T(8,128)(2,1)S(1)}, bf16[1024,64]{0,1:T(8,128)(2,1)}, u32[]{:S(2)}) copy-start(bf16[1024,64]{0,1:T(8,128)(2,1)} %get-tuple-element.360) | copy-start | bytes 393220
  1013.7 23.0 %copy-start.9 = (f32[4,64]{1,0:T(4,128)S(1)}, f32[4,64]{1,0:T(4,128)}, u32[]{:S(2)}) copy-start(f32[4,64]{1,0:T(4,128)} %get-tuple-element.401) | copy-start | bytes 3076
  1013.7 23.1 %copy-start.10 = (f32[4,64]{1,0:T(4,128)S(1)}, f32[4,64]{1,0:T(4,128)}, u32[]{:S(2)}) copy-start(f32[4,64]{1,0:T(4,128)} %get-tuple-element.402) | copy-start | bytes 3076
  1013.7 23.2 %copy-start.14 = (s32[2]{0:T(128)S(1)}, s32[2]{0:T(128)}, u32[]{:S(2)}) copy-start(s32[2]{0:T(128)} %iota_multiply_fusion) | copy-start | bytes 28
  1047.9 3.3 copy-start
  1070.0 3.3 copy-start
  1081.1 7.3 copy-start.6
  1082.2 2.0 collective-permute-start.12
  1085.5 25.7 %collective-permute-start.13 = (bf16[2,2,128,512]{3,2,1,0:T(8,128)(2,1)S(1)}, bf16[2,2,128,512]{3,2,1,0:T(8,128)(2,1)S(1)}, u32[]{:S(2)}, u32[]{:S(2)}) collective-permute-start(bf16[2,2,128,512]{3,2,1,0:T(8,128)(2,1)S(1)} %bitcast.210), channel_id=1, source_target_pairs={{0,2},{1,3},{2,0},{3,1},{4,6},{5,7},{6,4},{7,5},{8,10},{9,11},{10,... | collective-permute-start | bytes 1572872 | tf_op jit(solution)/shard_map/ppermute | solution.py:20
  1090.9 24.5 %collective-permute-start.16 = (bf16[2,2,128,256]{3,2,1,0:T(8,128)(2,1)}, bf16[2,2,128,256]{3,2,1,0:T(8,128)(2,1)}, u32[]{:S(2)}, u32[]{:S(2)}) collective-permute-start(bf16[2,2,128,256]{3,2,1,0:T(8,128)(2,1)} %bitcast.55), channel_id=1, source_target_pairs={{0,1},{1,0},{2,3},{3,2},{4,5},{5,4},{6,7},{7,6},{8,9},{9,8},{10,11... | collective-permute-start | bytes 786440 | tf_op jit(solution)/shard_map/ppermute | solution.py:20
  1111.3 18.2 %collective-permute-start.14 = (bf16[2,2,128,512]{3,2,1,0:T(8,128)(2,1)S(1)}, bf16[2,2,128,512]{3,2,1,0:T(8,128)(2,1)S(1)}, u32[]{:S(2)}, u32[]{:S(2)}) collective-permute-start(bf16[2,2,128,512]{3,2,1,0:T(8,128)(2,1)S(1)} %fusion.31), channel_id=1, source_target_pairs={{0,4},{1,5},{2,6},{3,7},{4,0},{5,1},{6,2},{7,3},{8,12},{9,13},{10,... | collective-permute-start | bytes 1572872 | tf_op jit(solution)/shard_map/ppermute | solution.py:20
  1117.2 32.3 %collective-permute-start.17 = (bf16[2,2,128,256]{3,2,1,0:T(8,128)(2,1)}, bf16[2,2,128,256]{3,2,1,0:T(8,128)(2,1)}, u32[]{:S(2)}, u32[]{:S(2)}) collective-permute-start(bf16[2,2,128,256]{3,2,1,0:T(8,128)(2,1)} %bitcast.176), channel_id=1, source_target_pairs={{0,2},{1,3},{2,0},{3,1},{4,6},{5,7},{6,4},{7,5},{8,10},{9,11},{10,... | collective-permute-start | bytes 786440 | tf_op jit(solution)/shard_map/ppermute | solution.py:20
  1130.9 56.5 %collective-permute-start.15 = (bf16[128,4096]{1,0:T(8,128)(2,1)S(1)}, bf16[128,4096]{1,0:T(8,128)(2,1)S(1)}, u32[]{:S(2)}, u32[]{:S(2)}) collective-permute-start(bf16[128,4096]{1,0:T(8,128)(2,1)S(1)} %copy.230), channel_id=1, source_target_pairs={{0,128},{128,0},{1,129},{129,1},{2,130},{130,2},{3,131},{131,3},{4... | collective-permute-start | bytes 3145736 | tf_op jit(solution)/shard_map/ppermute | solution.py:20
  1150.5 35.9 %collective-permute-start.18 = (bf16[2,2,128,256]{3,2,1,0:T(8,128)(2,1)S(1)}, bf16[2,2,128,256]{3,2,1,0:T(8,128)(2,1)S(1)}, u32[]{:S(2)}, u32[]{:S(2)}) collective-permute-start(bf16[2,2,128,256]{3,2,1,0:T(8,128)(2,1)S(1)} %fusion.41), channel_id=1, source_target_pairs={{0,4},{1,5},{2,6},{3,7},{4,0},{5,1},{6,2},{7,3},{8,12},{9,13},{10,... | collective-permute-start | bytes 786440 | tf_op jit(solution)/shard_map/ppermute | solution.py:20
Sparse Core Ops, SparseCore 0:
  675.7 337.8 all-gather.2
